TPU v7x, 512 devices: a whole 4x8x8 slice. The times are simulated.
512 devices in a mesh: ens: 32 (over z, y_lo, core), pen: 16 (over x, y_hi).
Axes of the slice: x: 4, y: 8 (y_hi: 4, y_lo: 2; y = y_hi * 2 + y_lo), z: 8, core: 2. Of those that a mesh axis runs over, the one named last changes fastest.
Arguments:
- state: float32 [2, 32, 4, 256, 512], P(None, 'ens', None, 'pen'), may hold values from -8 to 8, as said below
- accum: float32 [2, 32, 4, 256, 512], P(None, 'ens', None, 'pen'), may hold values from -8 to 8, as said below
- base_flow: float32 [6, 4, 256, 256], P(None, None, 'pen', 'ens'), may hold values from -6 to 6
Outputs:
- state_next: float32 [2, 32, 4, 256, 512], P(None, 'ens', None, 'pen')
- accum_next: float32 [2, 32, 4, 256, 512], P(None, 'ens', None, 'pen')
Inputs may be any that keep to these rules, and one draw needn't show every extreme that they name: `state`: each field of each perturbation and level is the spectrum of a real field: the entry at ((256 - ky) mod 256, (256 - kx) mod 256) is the complex conjugate of the entry at (ky, kx). `accum`: each field of each perturbation and level is the spectrum of a real field: the entry at ((256 - ky) mod 256, (256 - kx) mod 256) is the complex conjugate of the entry at (ky, kx).
All inputs are finite; a program needn't handle non-finite values.
Results may differ from a plain program's by a relative error of at most 0.0003.
Values sent between devices are 32-bit elements; how exact they have to be, the bound alone decides.
A program may use at most 64 MiB of HBM per device.

v0:
```python
import math
import jax
import jax.numpy as jnp
from jax import lax
from jax.sharding import PartitionSpec as P

viscosity = 0.05
diffusivity = 0.05
vertical_mixing = 0.5
buoyancy_gain = 0.5
stratification = 0.5
memory_factor = -5.0 / 9.0
weight_factor = 15.0 / 16.0
time_step = 0.4


def wave_numbers(amount, offset, length):
    position = offset + jnp.arange(amount, dtype=jnp.int32)
    half_length = length // 2
    signed = jnp.where(position <= half_length, position, position - length)
    derivative = jnp.where(position == half_length, 0, signed)
    return (2.0 * math.pi / length * derivative.astype(jnp.float32), signed)


def times_i(real_part, imag_part, factor):
    return (-factor * imag_part, factor * real_part)


def vertical(quantity, level_axis):
    depth = quantity.shape[level_axis]
    lower = lax.slice_in_dim(quantity, 0, 1, axis=level_axis)
    upper = lax.slice_in_dim(quantity, depth - 1, depth, axis=level_axis)
    padded = jnp.concatenate([lower, quantity, upper], axis=level_axis)
    above = lax.slice_in_dim(padded, 2, depth + 2, axis=level_axis)
    below = lax.slice_in_dim(padded, 0, depth, axis=level_axis)
    return above + below - 2.0 * quantity


def tendency(vort, buoy, advect, across, kappa_x, square, level_axis):
    tend_vort_re = (
        -advect[0]
        + buoyancy_gain * (-kappa_x * buoy[1])
        - viscosity * square * vort[0]
        + vertical_mixing * vertical(vort[0], level_axis)
    )
    tend_vort_im = (
        -advect[1]
        + buoyancy_gain * (kappa_x * buoy[0])
        - viscosity * square * vort[1]
        + vertical_mixing * vertical(vort[1], level_axis)
    )
    tend_buoy_re = (
        -advect[2]
        - stratification * across[0]
        - diffusivity * square * buoy[0]
        + vertical_mixing * vertical(buoy[0], level_axis)
    )
    tend_buoy_im = (
        -advect[3]
        - stratification * across[1]
        - diffusivity * square * buoy[1]
        + vertical_mixing * vertical(buoy[1], level_axis)
    )
    return jnp.stack(
        [
            jnp.concatenate([tend_vort_re, tend_vort_im], axis=-1),
            jnp.concatenate([tend_buoy_re, tend_buoy_im], axis=-1),
        ]
    )


def dft_tables(length):
    position = jnp.arange(length, dtype=jnp.int32)
    product = position[:, None] * position[None, :] % length
    angle = 2.0 * math.pi / length * product.astype(jnp.float32)
    scale = 1.0 / math.sqrt(length)
    return (scale * jnp.cos(angle), scale * jnp.sin(angle))


def to_physical(spectral, x_table, y_table):
    mixed_space = jnp.einsum(
        "fplkj,jcx->fplcxk", spectral, x_table, precision=lax.Precision.HIGHEST
    )
    return jnp.einsum(
        "fplcxk,ckm->fplxm",
        lax.all_to_all(mixed_space, "pen", split_axis=4, concat_axis=5, tiled=True),
        y_table,
        precision=lax.Precision.HIGHEST,
    )


def on_device(state, accum, base_flow):
    grid_size = state.shape[-1] // 2
    row_count = state.shape[3]
    base_all = lax.all_gather(base_flow, "ens", axis=3, tiled=True)
    kappa_rows, signed_y = wave_numbers(row_count, lax.axis_index("pen") * row_count, grid_size)
    kappa_cols, signed_x = wave_numbers(grid_size, 0, grid_size)
    kappa_y = kappa_rows[:, None]
    kappa_x = kappa_cols[None, :]
    wave_square = signed_y[:, None] ** 2 + signed_x[None, :] ** 2
    factor = (2.0 * math.pi / grid_size) ** 2
    square = factor * wave_square.astype(jnp.float32)
    inverse = jnp.where(
        wave_square > 0, 1.0 / (factor * jnp.maximum(wave_square, 1).astype(jnp.float32)), 0.0
    )
    vort = (state[0][..., :grid_size], state[0][..., grid_size:])
    buoy = (state[1][..., :grid_size], state[1][..., grid_size:])
    potential_re = -vort[0] * inverse
    potential_im = -vort[1] * inverse
    flow_x = times_i(potential_re, potential_im, -kappa_y)
    flow_y = times_i(potential_re, potential_im, kappa_x)
    vort_x = times_i(vort[0], vort[1], kappa_x)
    vort_y = times_i(vort[0], vort[1], kappa_y)
    buoy_x = times_i(buoy[0], buoy[1], kappa_x)
    buoy_y = times_i(buoy[0], buoy[1], kappa_y)
    cosine_table, sine_table = dft_tables(grid_size)
    x_table = jnp.concatenate(
        [
            jnp.stack([cosine_table, sine_table], axis=1),
            jnp.stack([-sine_table, cosine_table], axis=1),
        ],
        axis=0,
    )
    y_table = jnp.stack([cosine_table, -sine_table])
    components = [flow_x, flow_y, vort_x, vort_y, buoy_x, buoy_y]
    spectral = jnp.stack([jnp.concatenate(component, axis=-1) for component in components])
    physical = to_physical(spectral, x_table, y_table)
    flow_x_p, flow_y_p = (physical[0], physical[1])
    vort_x_p, vort_y_p = (physical[2], physical[3])
    buoy_x_p, buoy_y_p = (physical[4], physical[5])
    advect_vort = (
        base_all[0] * vort_x_p
        + base_all[1] * vort_y_p
        + flow_x_p * base_all[2]
        + flow_y_p * base_all[3]
    )
    advect_buoy = (
        base_all[0] * buoy_x_p
        + base_all[1] * buoy_y_p
        + flow_x_p * base_all[4]
        + flow_y_p * base_all[5]
    )
    advect_both = jnp.stack([advect_vort, advect_buoy])
    y_forward = jnp.stack([cosine_table, -sine_table], axis=1)
    x_forward = jnp.stack(
        [
            jnp.concatenate([cosine_table, -sine_table], axis=1),
            jnp.concatenate([sine_table, cosine_table], axis=1),
        ]
    )
    spread = jnp.einsum(
        "fplxy,yck->fplckx", advect_both, y_forward, precision=lax.Precision.HIGHEST
    )
    spectra = jnp.einsum(
        "fplckx,cxm->fplkm",
        lax.all_to_all(spread, "pen", split_axis=4, concat_axis=5, tiled=True),
        x_forward,
        precision=lax.Precision.HIGHEST,
    )
    advect = (
        spectra[0][..., :grid_size],
        spectra[0][..., grid_size:],
        spectra[1][..., :grid_size],
        spectra[1][..., grid_size:],
    )
    tend = tendency(vort, buoy, advect, flow_y, kappa_x, square, 1)
    accum_next = memory_factor * accum + tend
    state_next = state + weight_factor * time_step * accum_next
    return (state_next, accum_next)


def solution(mesh):
    return jax.shard_map(
        on_device,
        mesh=mesh,
        in_specs=(
            P(None, "ens", None, "pen", None),
            P(None, "ens", None, "pen", None),
            P(None, None, "pen", "ens"),
        ),
        out_specs=(P(None, "ens", None, "pen", None), P(None, "ens", None, "pen", None)),
        check_vma=False,
    )
```

profile of v0, /device:TPU:1, one launch (start us, length us, event | category | flops | bytes accessed | tf_op | source)
XLA Modules:
  0.0 172.0 jit_solution(4518188159568962184)
XLA Ops:
  0.7 1.1 sine_multiply_fusion.1
  1.7 1.0 fusion.39
  2.7 1.1 slice_bitcast_fusion.1
  3.8 0.1 fusion.81
  3.9 0.6 copy-done.4
  4.5 0.7 fusion.97
  5.2 0.7 fusion.73
  6.0 0.5 copy-done.5
  6.5 0.0 copy-done.7
  6.5 1.5 convolution_bitcast_fusion
  8.0 5.0 %copy.20 = f32[6,1,4,2,256,16]{5,2,0,3,1,4:T(4,128)} copy(f32[6,1,4,2,256,16]{4,5,2,0,3,1:T(8,128)S(1)} %convolution_bitcast_fusion) | data formatting | bytes 1572864 | tf_op jit(solution)/shard_map/fplkj,jcx->fplcxk/transpose | solution.py:81
  13.0 7.2 %reshape.338 = f32[16,1,12288]{2,1,0:T(1,128)} reshape(f32[256,1,2,6,4,16]{5,4,3,2,1,0:T(4,128)} %bitcast.114) | data formatting | bytes 1572864
  20.2 10.2 %all-to-all-start = ((f32[16,1,12288]{2,1,0:T(1,128)}), f32[16,1,12288]{2,1,0:T(1,128)S(1)}, u32[]{:S(2)}, u32[]{:S(2)}) async-start(f32[16,1,12288]{2,1,0:T(1,128)} %reshape.338), calls=%async_computation | async-start | bytes 1572864 | tf_op jit(solution)/shard_map/all_to_all | solution.py:86
  30.5 71.0 %all_gather.3 = f32[6,4,16,256]{2,1,0,3:T(4,128)S(1)} all-gather(f32[6,4,16,8]{2,1,0,3:T(4,128)S(1)} %copy.13), channel_id=1, replica_groups=mesh['ens'=32,'pen'=16] {'ens'}, dimensions={3}, use_global_device_ids=true | all-gather | bytes 405504 | tf_op jit(solution)/shard_map/all_gather | solution.py:95
  101.4 1.5 fusion.94
  102.9 1.8 %copy.35 = f32[1,4,16,256]{3,2,1,0:T(8,128)} copy(f32[1,4,16,256]{2,1,0,3:T(4,128)} %get-tuple-element.8) | data formatting | bytes 131072
  104.8 1.8 %copy.36 = f32[1,4,16,256]{3,2,1,0:T(8,128)} copy(f32[1,4,16,256]{2,1,0,3:T(4,128)} %get-tuple-element.7) | data formatting | bytes 131072
  106.6 0.8 copy.37
  107.4 0.8 copy.38
  108.2 0.2 copy.39
  108.4 0.2 copy.40
  108.6 1.7 fusion.40
  110.3 1.1 multiply_negate_fusion
  111.4 0.5 broadcast.510
  111.9 2.4 %reduce = f32[16,12288]{1,0:T(8,128)S(1)} reduce(f32[16,1,12288]{2,1,0:T(1,128)S(1)} %all-to-all-done, f32[]{:T(128)} %broadcast.510), dimensions={1}, to_apply=%all_to_all.22.reduce_sub_computation | reduce | bytes 1572868 | tf_op jit(solution)/shard_map/all_to_all | solution.py:86
  114.3 6.3 %reshape.339 = f32[256,1,2,6,4,16]{5,4,3,2,1,0:T(4,128)} reshape(f32[16,12288]{1,0:T(8,128)S(1)} %reduce) | data formatting | bytes 1572864
  120.6 9.1 %copy.43 = f32[6,1,4,2,16,16,16]{6,4,5,3,2,0,1:T(8,128)} copy(f32[6,1,4,2,16,16,16]{6,2,0,3,5,4,1:T(4,128)} %bitcast.115) | data formatting | bytes 1572864 | tf_op jit(solution)/shard_map/all_to_all | solution.py:86
  129.7 0.0 copy-start.2
  129.7 4.9 %reshape.327 = f32[6,4,2,16,256]{4,3,2,1,0:T(8,128)S(1)} reshape(f32[6,1,4,2,16,16,16]{6,5,4,3,2,0,1:T(8,128)} %bitcast.116) | data formatting | bytes 1572864 | tf_op jit(solution)/shard_map/reshape.16
  134.7 0.8 convolution_bitcast_fusion.1
  135.5 0.1 fusion.72
  135.6 0.4 convolution_bitcast_fusion.2
  136.0 1.3 copy.27
  137.3 2.3 %reshape.340 = f32[16,1,4096]{2,1,0:T(1,128)} reshape(f32[256,1,2,2,4,16]{5,4,3,2,1,0:T(4,128)S(1)} %bitcast.117) | data formatting | bytes 524288
  139.6 9.8 %all-to-all-start.1 = ((f32[16,1,4096]{2,1,0:T(1,128)}), f32[16,1,4096]{2,1,0:T(1,128)S(1)}, u32[]{:S(2)}, u32[]{:S(2)}) async-start(f32[16,1,4096]{2,1,0:T(1,128)} %reshape.340), calls=%async_computation.1 | async-start | bytes 524288 | tf_op jit(solution)/shard_map/all_to_all | solution.py:156
  149.4 1.1 sine_multiply_fusion
  150.4 0.1 maximum_bitcast_fusion.8
  150.6 1.4 fusion.95
  152.0 10.0 %all-to-all-done.1 = f32[16,1,4096]{2,1,0:T(1,128)S(1)} async-done(((f32[16,1,4096]{2,1,0:T(1,128)}), f32[16,1,4096]{2,1,0:T(1,128)S(1)}, u32[]{:S(2)}, u32[]{:S(2)}) %all-to-all-start.1) | async-done | bytes 262176 | tf_op jit(solution)/shard_map/all_to_all | solution.py:156
  162.0 1.2 reduce.1
  163.2 1.5 reshape.341
  164.8 2.6 %copy.44 = f32[2,1,4,2,16,16,16]{6,4,5,3,2,0,1:T(8,128)} copy(f32[2,1,4,2,16,16,16]{6,2,0,3,5,4,1:T(4,128)S(1)} %bitcast.118) | data formatting | bytes 524288 | tf_op jit(solution)/shard_map/all_to_all | solution.py:156
  167.4 0.0 copy-start.23
  167.4 2.6 %reshape.329 = f32[2,4,2,16,256]{4,3,2,1,0:T(8,128)S(1)} reshape(f32[2,1,4,2,16,16,16]{6,5,4,3,2,0,1:T(8,128)} %bitcast.119) | data formatting | bytes 524288 | tf_op jit(solution)/shard_map/reshape.33
  170.0 0.7 convolution_bitcast_fusion.3
  170.8 0.1 fusion.56
  171.0 0.1 fusion.62
  171.1 0.9 multiply_add_fusion
  (71 shorter events, 0.3 us)
Async XLA Ops:
  2.7 3.8 %copy-start.1 = (f32[256,1,256]{2,0,1:T(8,128)}, f32[256,1,256]{2,0,1:T(8,128)S(1)}, u32[]{:S(2)}) copy-start(f32[256,1,256]{2,0,1:T(8,128)S(1)} %fusion.39) | copy-start | bytes 786436
  3.8 0.7 copy-start.4
  5.1 0.8 copy-start.9
  5.1 0.8 copy-start.11
  5.9 0.6 copy-start.5
  5.9 0.7 copy-start.7
  13.0 17.4 %copy-start.22 = (f32[6,4,16,8]{2,3,1,0:T(8,128)S(1)}, f32[6,4,16,8]{2,3,1,0:T(8,128)}, u32[]{:S(2)}) copy-start(f32[6,4,16,8]{2,3,1,0:T(8,128)} %param.5) | copy-start | bytes 36868
  20.2 91.2 %all-to-all-start = ((f32[16,1,12288]{2,1,0:T(1,128)}), f32[16,1,12288]{2,1,0:T(1,128)S(1)}, u32[]{:S(2)}, u32[]{:S(2)}) async-start(f32[16,1,12288]{2,1,0:T(1,128)} %reshape.338), calls=%async_computation | async-start | bytes 1572864 | tf_op jit(solution)/shard_map/all_to_all | solution.py:86
  129.7 5.8 %copy-start.13 = (f32[1,4,16,256]{3,2,1,0:T(8,128)S(1)}, f32[1,4,16,256]{3,2,1,0:T(8,128)}, u32[]{:S(2)}) copy-start(f32[1,4,16,256]{3,2,1,0:T(8,128)} %copy.35) | copy-start | bytes 196612
  129.7 5.8 %copy-start.14 = (f32[1,4,16,256]{3,2,1,0:T(8,128)S(1)}, f32[1,4,16,256]{3,2,1,0:T(8,128)}, u32[]{:S(2)}) copy-start(f32[1,4,16,256]{3,2,1,0:T(8,128)} %copy.36) | copy-start | bytes 196612
  129.7 5.8 %copy-start.15 = (f32[1,4,16,256]{3,2,1,0:T(8,128)S(1)}, f32[1,4,16,256]{3,2,1,0:T(8,128)}, u32[]{:S(2)}) copy-start(f32[1,4,16,256]{3,2,1,0:T(8,128)} %copy.37) | copy-start | bytes 196612
  129.7 5.8 %copy-start.16 = (f32[1,4,16,256]{3,2,1,0:T(8,128)S(1)}, f32[1,4,16,256]{3,2,1,0:T(8,128)}, u32[]{:S(2)}) copy-start(f32[1,4,16,256]{3,2,1,0:T(8,128)} %copy.38) | copy-start | bytes 196612
  129.7 5.9 %copy-start.2 = (f32[256,1,256]{2,0,1:T(8,128)S(1)}, f32[256,1,256]{2,0,1:T(8,128)}, u32[]{:S(2)}) copy-start(f32[256,1,256]{2,0,1:T(8,128)} %copy-done.1) | copy-start | bytes 786436
  136.0 14.4 %copy-start.3 = (f32[256,256]{1,0:T(8,128)S(1)}, f32[256,256]{1,0:T(8,128)}, u32[]{:S(2)}) copy-start(f32[256,256]{1,0:T(8,128)} %fusion.40) | copy-start | bytes 786436
  139.6 22.4 %all-to-all-start.1 = ((f32[16,1,4096]{2,1,0:T(1,128)}), f32[16,1,4096]{2,1,0:T(1,128)S(1)}, u32[]{:S(2)}, u32[]{:S(2)}) async-start(f32[16,1,4096]{2,1,0:T(1,128)} %reshape.340), calls=%async_computation.1 | async-start | bytes 524288 | tf_op jit(solution)/shard_map/all_to_all | solution.py:156
  164.7 6.0 %copy-start.8 = (f32[1,4,16,256]{3,2,1,0:T(8,128)S(1)}, f32[1,4,16,256]{3,2,1,0:T(8,128)}, u32[]{:S(2)}) copy-start(f32[1,4,16,256]{3,2,1,0:T(8,128)} %copy-done.7) | copy-start | bytes 196612
  164.7 6.0 %copy-start.12 = (f32[1,4,16,256]{3,2,1,0:T(8,128)S(1)}, f32[1,4,16,256]{3,2,1,0:T(8,128)}, u32[]{:S(2)}) copy-start(f32[1,4,16,256]{3,2,1,0:T(8,128)} %copy-done.11) | copy-start | bytes 196612
  164.7 6.0 %copy-start.19 = (f32[1,4,16,256]{3,2,1,0:T(8,128)S(1)}, f32[1,4,16,256]{3,2,1,0:T(8,128)}, u32[]{:S(2)}) copy-start(f32[1,4,16,256]{3,2,1,0:T(8,128)} %get-tuple-element.29) | copy-start | bytes 196612
  164.7 6.0 %copy-start.21 = (f32[1,4,16,256]{3,2,1,0:T(8,128)S(1)}, f32[1,4,16,256]{3,2,1,0:T(8,128)}, u32[]{:S(2)}) copy-start(f32[1,4,16,256]{3,2,1,0:T(8,128)} %get-tuple-element.38) | copy-start | bytes 196612
  164.8 6.0 %copy-start.27 = (f32[1,1,16,256]{3,2,1,0:T(8,128)S(1)}, f32[1,1,16,256]{3,2,1,0:T(8,128)}, u32[]{:S(2)}) copy-start(f32[1,1,16,256]{3,2,1,0:T(8,128)} %get-tuple-element.31) | copy-start | bytes 49156
  164.8 6.0 %copy-start.28 = (f32[1,1,16,256]{3,2,1,0:T(8,128)S(1)}, f32[1,1,16,256]{3,2,1,0:T(8,128)}, u32[]{:S(2)}) copy-start(f32[1,1,16,256]{3,2,1,0:T(8,128)} %get-tuple-element.32) | copy-start | bytes 49156
  164.8 6.0 %copy-start.29 = (f32[1,1,16,256]{3,2,1,0:T(8,128)S(1)}, f32[1,1,16,256]{3,2,1,0:T(8,128)}, u32[]{:S(2)}) copy-start(f32[1,1,16,256]{3,2,1,0:T(8,128)} %get-tuple-element.48) | copy-start | bytes 49156
  164.8 6.0 %copy-start.30 = (f32[1,1,16,256]{3,2,1,0:T(8,128)S(1)}, f32[1,1,16,256]{3,2,1,0:T(8,128)}, u32[]{:S(2)}) copy-start(f32[1,1,16,256]{3,2,1,0:T(8,128)} %get-tuple-element.51) | copy-start | bytes 49156
  167.4 3.5 %copy-start.6 = (f32[1,4,16,256]{3,2,1,0:T(8,128)S(1)}, f32[1,4,16,256]{3,2,1,0:T(8,128)}, u32[]{:S(2)}) copy-start(f32[1,4,16,256]{3,2,1,0:T(8,128)} %copy-done.5) | copy-start | bytes 196612
  167.4 3.5 %copy-start.10 = (f32[1,4,16,256]{3,2,1,0:T(8,128)S(1)}, f32[1,4,16,256]{3,2,1,0:T(8,128)}, u32[]{:S(2)}) copy-start(f32[1,4,16,256]{3,2,1,0:T(8,128)} %copy-done.9) | copy-start | bytes 196612
  167.4 3.5 %copy-start.18 = (f32[1,4,16,256]{3,2,1,0:T(8,128)S(1)}, f32[1,4,16,256]{3,2,1,0:T(8,128)}, u32[]{:S(2)}) copy-start(f32[1,4,16,256]{3,2,1,0:T(8,128)} %get-tuple-element.28) | copy-start | bytes 196612
  167.4 3.5 %copy-start.20 = (f32[1,4,16,256]{3,2,1,0:T(8,128)S(1)}, f32[1,4,16,256]{3,2,1,0:T(8,128)}, u32[]{:S(2)}) copy-start(f32[1,4,16,256]{3,2,1,0:T(8,128)} %get-tuple-element.43) | copy-start | bytes 196612
  167.4 3.6 %copy-start.23 = (f32[1,1,16,256]{3,2,1,0:T(8,128)S(1)}, f32[1,1,16,256]{3,2,1,0:T(8,128)}, u32[]{:S(2)}) copy-start(f32[1,1,16,256]{3,2,1,0:T(8,128)} %get-tuple-element.30) | copy-start | bytes 49156
  167.4 3.6 %copy-start.24 = (f32[1,1,16,256]{3,2,1,0:T(8,128)S(1)}, f32[1,1,16,256]{3,2,1,0:T(8,128)}, u32[]{:S(2)}) copy-start(f32[1,1,16,256]{3,2,1,0:T(8,128)} %get-tuple-element.33) | copy-start | bytes 49156
  167.4 3.6 %copy-start.25 = (f32[1,1,16,256]{3,2,1,0:T(8,128)S(1)}, f32[1,1,16,256]{3,2,1,0:T(8,128)}, u32[]{:S(2)}) copy-start(f32[1,1,16,256]{3,2,1,0:T(8,128)} %get-tuple-element.49) | copy-start | bytes 49156
  167.4 3.6 %copy-start.26 = (f32[1,1,16,256]{3,2,1,0:T(8,128)S(1)}, f32[1,1,16,256]{3,2,1,0:T(8,128)}, u32[]{:S(2)}) copy-start(f32[1,1,16,256]{3,2,1,0:T(8,128)} %get-tuple-element.50) | copy-start | bytes 49156
  167.4 3.6 %copy-start = (f32[2,1,4,16,512]{4,3,2,1,0:T(8,128)S(1)}, f32[2,1,4,16,512]{4,3,2,1,0:T(8,128)}, u32[]{:S(2)}) copy-start(f32[2,1,4,16,512]{4,3,2,1,0:T(8,128)} %param.3) | copy-start | bytes 786436
  167.4 3.6 %copy-start.17 = (f32[2,1,4,16,512]{4,3,2,1,0:T(8,128)S(1)}, f32[2,1,4,16,512]{4,3,2,1,0:T(8,128)}, u32[]{:S(2)}) copy-start(f32[2,1,4,16,512]{4,3,2,1,0:T(8,128)} %param.4) | copy-start | bytes 786436
where the time goes:
time: 173 us; the launch traced here: 172 us
  blocking collectives  71 us (41%)
  local copies, waits for them, and re-layouts  54.2 us (31%)
  starting transfers between devices  20 us (12%)
  other arithmetic  12.2 us (7%)
  waiting for transfers between devices  10 us (6%)
  matrix products  3.41 us (2%)
    all_gather x1, blocking collectives, on_device(): base_all = lax.all_gather(base_flow, 'ens', axis=3, tiled=True)  71 us
    unnamed x73, local copies, waits for them, and re-layouts  24.2 us
    all_to_all x1, starting transfers between devices, to_physical(): lax.all_to_all(mixed_space, 'pen', split_axis=4, concat_axis=5, tiled=True)  10.2 us
    all_to_all x1, waiting for transfers between devices, on_device(): lax.all_to_all(spread, 'pen', split_axis=4, concat_axis=5, tiled=True)  10 us
    all_to_all x1, starting transfers between devices, on_device(): lax.all_to_all(spread, 'pen', split_axis=4, concat_axis=5, tiled=True)  9.75 us
    all_to_all x2, local copies, waits for them, and re-layouts, to_physical(): lax.all_to_all(mixed_space, 'pen', split_axis=4, concat_axis=5, tiled=True)  9.59 us
    another operation x2, local copies, waits for them, and re-layouts  7.5 us
    transpose x1, local copies, waits for them, and re-layouts, to_physical(): jnp.einsum('fplkj,jcx->fplcxk', spectral, x_table, precision=lax.Precisio...  4.97 us
  transfers between devices with their start and end apart: 2, of which 1 were waited for; matrix products, arithmetic and copies ran while one was open for 7% of the time, Pallas kernels for 0%

commit v1 on v0

--- a/solution.py
+++ b/solution.py
@@ -12,6 +12,13 @@
 memory_factor = -5.0 / 9.0
 weight_factor = 15.0 / 16.0
 time_step = 0.4
+
+
+def stacked_exchange(x, axis, split, join):
+    size = lax.axis_size(axis)
+    blocks = jnp.stack(jnp.split(x, size, axis=split), axis=0)
+    blocks = lax.all_to_all(blocks, axis, split_axis=0, concat_axis=0)
+    return jnp.concatenate(blocks, axis=join)
 
 
 def wave_numbers(amount, offset, length):
@@ -153,7 +160,7 @@
     )
     spectra = jnp.einsum(
         "fplckx,cxm->fplkm",
-        lax.all_to_all(spread, "pen", split_axis=4, concat_axis=5, tiled=True),
+        stacked_exchange(spread, "pen", 4, 5),
         x_forward,
         precision=lax.Precision.HIGHEST,
     )

time: 173 us -> 171 us (0.988)
  local copies, waits for them, and re-layouts: 54.2 us -> 50.6 us
    reshape x0 -> x2, local copies, waits for them, and re-layouts: none -> 3.7 us  [stacked_exchange(): return jnp.concatenate(blocks, axis=join)]
    all_to_all x1 -> x0, local copies, waits for them, and re-layouts: 2.57 us -> none  [on_device(): lax.all_to_all(spread, 'pen', split_axis=4, concat_axis=5, tiled=True)]
    another operation x2 -> x3, local copies, waits for them, and re-layouts: 7.5 us -> 5.94 us
    unnamed x73 -> x74, local copies, waits for them, and re-layouts: 24.2 us -> 23.3 us
where the time goes in v1:
time: 171 us; the launch traced here: 170 us
  blocking collectives  71 us (42%)
  local copies, waits for them, and re-layouts  50.6 us (30%)
  starting transfers between devices  20.1 us (12%)
  other arithmetic  13.2 us (8%)
  waiting for transfers between devices  10.8 us (6%)
  matrix products  3.41 us (2%)
    all_gather x1, blocking collectives, on_device(): base_all = lax.all_gather(base_flow, 'ens', axis=3, tiled=True)  71 us
    unnamed x74, local copies, waits for them, and re-layouts  23.3 us
    all_to_all x1, waiting for transfers between devices, stacked_exchange(): blocks = lax.all_to_all(blocks, axis, split_axis=0, concat_axis=0)  10.8 us
    all_to_all x1, starting transfers between devices, to_physical(): lax.all_to_all(mixed_space, 'pen', split_axis=4, concat_axis=5, tiled=True)  10.2 us
    all_to_all x1, starting transfers between devices, stacked_exchange(): blocks = lax.all_to_all(blocks, axis, split_axis=0, concat_axis=0)  9.88 us
    all_to_all x2, local copies, waits for them, and re-layouts, to_physical(): lax.all_to_all(mixed_space, 'pen', split_axis=4, concat_axis=5, tiled=True)  9.55 us
    another operation x2, local copies, waits for them, and re-layouts  5.84 us
    transpose x1, local copies, waits for them, and re-layouts, to_physical(): jnp.einsum('fplkj,jcx->fplcxk', spectral, x_table, precision=lax.Precisio...  4.95 us
  transfers between devices with their start and end apart: 2, of which 1 were waited for; matrix products, arithmetic and copies ran while one was open for 7% of the time, Pallas kernels for 0%

profile of v1, /device:TPU:1, one launch (start us, length us, event | category | flops | bytes accessed | tf_op | source)
XLA Modules:
  0.0 170.4 jit_solution(15799575634628017590)
XLA Ops:
  0.7 1.1 sine_multiply_fusion.1
  1.7 1.0 fusion.55
  2.7 1.1 slice_bitcast_fusion.17
  3.9 0.6 copy-done.4
  4.5 0.7 fusion.113
  5.2 0.7 fusion.89
  6.0 0.5 copy-done.6
  6.5 1.5 convolution_bitcast_fusion
  8.0 4.9 %copy.27 = f32[6,1,4,2,256,16]{5,2,0,3,1,4:T(4,128)} copy(f32[6,1,4,2,256,16]{4,5,2,0,3,1:T(8,128)S(1)} %convolution_bitcast_fusion) | data formatting | bytes 1572864 | tf_op jit(solution)/shard_map/fplkj,jcx->fplcxk/transpose | solution.py:88
  12.9 7.2 %reshape.343 = f32[16,1,12288]{2,1,0:T(1,128)} reshape(f32[256,1,2,6,4,16]{5,4,3,2,1,0:T(4,128)} %bitcast.177) | data formatting | bytes 1572864
  20.2 10.2 %all-to-all-start = ((f32[16,1,12288]{2,1,0:T(1,128)}), f32[16,1,12288]{2,1,0:T(1,128)S(1)}, u32[]{:S(2)}, u32[]{:S(2)}) async-start(f32[16,1,12288]{2,1,0:T(1,128)} %reshape.343), calls=%async_computation | async-start | bytes 1572864 | tf_op jit(solution)/shard_map/all_to_all | solution.py:93
  30.4 71.0 %all_gather.3 = f32[6,4,16,256]{2,1,0,3:T(4,128)S(1)} all-gather(f32[6,4,16,8]{2,1,0,3:T(4,128)S(1)} %copy.20), channel_id=1, replica_groups=mesh['ens'=32,'pen'=16] {'ens'}, dimensions={3}, use_global_device_ids=true | all-gather | bytes 405504 | tf_op jit(solution)/shard_map/all_gather | solution.py:102
  101.4 1.5 fusion.110
  102.9 1.8 %copy.41 = f32[1,4,16,256]{3,2,1,0:T(8,128)} copy(f32[1,4,16,256]{2,1,0,3:T(4,128)} %get-tuple-element.8) | data formatting | bytes 131072
  104.7 1.8 %copy.42 = f32[1,4,16,256]{3,2,1,0:T(8,128)} copy(f32[1,4,16,256]{2,1,0,3:T(4,128)} %get-tuple-element.7) | data formatting | bytes 131072
  106.6 0.8 copy.43
  107.4 0.2 copy.44
  107.6 0.2 copy.45
  107.8 0.2 copy.46
  107.9 1.7 fusion.56
  109.6 1.1 multiply_negate_fusion
  110.7 0.5 broadcast.510
  111.2 2.4 %reduce = f32[16,12288]{1,0:T(8,128)S(1)} reduce(f32[16,1,12288]{2,1,0:T(1,128)S(1)} %all-to-all-done, f32[]{:T(128)} %broadcast.510), dimensions={1}, to_apply=%all_to_all.14.reduce_sub_computation | reduce | bytes 1572868 | tf_op jit(solution)/shard_map/all_to_all | solution.py:93
  113.7 6.3 %reshape.344 = f32[256,1,2,6,4,16]{5,4,3,2,1,0:T(4,128)} reshape(f32[16,12288]{1,0:T(8,128)S(1)} %reduce) | data formatting | bytes 1572864
  120.0 9.1 %copy.48 = f32[6,1,4,2,16,16,16]{6,4,5,3,2,0,1:T(8,128)} copy(f32[6,1,4,2,16,16,16]{6,2,0,3,5,4,1:T(4,128)} %bitcast.178) | data formatting | bytes 1572864 | tf_op jit(solution)/shard_map/all_to_all | solution.py:93
  129.0 4.9 %reshape.331 = f32[6,4,2,16,256]{4,3,2,1,0:T(8,128)S(1)} reshape(f32[6,1,4,2,16,16,16]{6,5,4,3,2,0,1:T(8,128)} %bitcast.179) | data formatting | bytes 1572864 | tf_op jit(solution)/shard_map/reshape.18
  134.0 0.8 convolution_bitcast_fusion.1
  134.9 0.4 convolution_bitcast_fusion.2
  135.5 0.1 fusion.44
  135.6 0.1 fusion.43
  135.7 0.1 fusion.42
  135.8 0.1 fusion.41
  135.9 0.1 fusion.40
  136.4 0.1 fusion.34
  136.8 1.5 reshape.345
  138.3 9.9 %all-to-all-start.1 = ((f32[16,1,4096]{2,1,0:T(1,128)}), f32[16,1,4096]{2,1,0:T(1,128)S(1)}, u32[]{:S(2)}, u32[]{:S(2)}) async-start(f32[16,1,4096]{2,1,0:T(1,128)} %reshape.345), calls=%async_computation.1 | async-start | bytes 524288 | tf_op jit(solution)/shard_map/all_to_all | solution.py:20
  148.2 1.1 sine_multiply_fusion
  149.3 0.1 maximum_bitcast_fusion.8
  149.4 0.6 fusion.111
  150.0 10.8 %all-to-all-done.1 = f32[16,1,4096]{2,1,0:T(1,128)S(1)} async-done(((f32[16,1,4096]{2,1,0:T(1,128)}), f32[16,1,4096]{2,1,0:T(1,128)S(1)}, u32[]{:S(2)}, u32[]{:S(2)}) %all-to-all-start.1) | async-done | bytes 262176 | tf_op jit(solution)/shard_map/all_to_all | solution.py:20
  160.8 1.2 reduce.1
  162.0 0.7 reshape.346
  162.7 1.5 bitcast_bitcast_fusion
  164.2 2.2 %copy.34 = f32[2,1,4,2,16,16,16]{6,5,4,3,2,0,1:T(8,128)S(1)} copy(f32[2,1,4,2,16,16,16]{4,6,2,0,3,1,5:T(8,128)} %bitcast_bitcast_fusion) | data formatting | bytes 524288 | tf_op jit(solution)/shard_map/reshape | solution.py:21
  166.5 0.9 reshape.334
  167.5 0.7 convolution_bitcast_fusion.3
  168.2 1.1 fusion.72
  169.5 0.9 multiply_add_fusion
  (73 shorter events, 1.3 us)
Async XLA Ops:
  2.7 3.8 %copy-start.1 = (f32[256,1,256]{2,0,1:T(8,128)}, f32[256,1,256]{2,0,1:T(8,128)S(1)}, u32[]{:S(2)}) copy-start(f32[256,1,256]{2,0,1:T(8,128)S(1)} %fusion.55) | copy-start | bytes 786436
  3.8 0.7 copy-start.4
  5.1 0.8 copy-start.10
  5.1 0.8 copy-start.12
  5.9 0.6 copy-start.6
  5.9 0.7 copy-start.8
  12.9 17.4 %copy-start.19 = (f32[6,4,16,8]{2,3,1,0:T(8,128)S(1)}, f32[6,4,16,8]{2,3,1,0:T(8,128)}, u32[]{:S(2)}) copy-start(f32[6,4,16,8]{2,3,1,0:T(8,128)} %param.5) | copy-start | bytes 36868
  20.2 90.5 %all-to-all-start = ((f32[16,1,12288]{2,1,0:T(1,128)}), f32[16,1,12288]{2,1,0:T(1,128)S(1)}, u32[]{:S(2)}, u32[]{:S(2)}) async-start(f32[16,1,12288]{2,1,0:T(1,128)} %reshape.343), calls=%async_computation | async-start | bytes 1572864 | tf_op jit(solution)/shard_map/all_to_all | solution.py:93
  129.0 5.7 %copy-start.13 = (f32[1,4,16,256]{3,2,1,0:T(8,128)S(1)}, f32[1,4,16,256]{3,2,1,0:T(8,128)}, u32[]{:S(2)}) copy-start(f32[1,4,16,256]{3,2,1,0:T(8,128)} %copy.41) | copy-start | bytes 196612
  129.0 5.7 %copy-start.14 = (f32[1,4,16,256]{3,2,1,0:T(8,128)S(1)}, f32[1,4,16,256]{3,2,1,0:T(8,128)}, u32[]{:S(2)}) copy-start(f32[1,4,16,256]{3,2,1,0:T(8,128)} %copy.42) | copy-start | bytes 196612
  129.0 5.7 %copy-start.15 = (f32[1,4,16,256]{3,2,1,0:T(8,128)S(1)}, f32[1,4,16,256]{3,2,1,0:T(8,128)}, u32[]{:S(2)}) copy-start(f32[1,4,16,256]{3,2,1,0:T(8,128)} %copy.43) | copy-start | bytes 196612
  133.9 1.0 copy-start.2
  136.5 12.7 %copy-start.3 = (f32[256,256]{1,0:T(8,128)S(1)}, f32[256,256]{1,0:T(8,128)}, u32[]{:S(2)}) copy-start(f32[256,256]{1,0:T(8,128)} %fusion.56) | copy-start | bytes 786436
  138.3 11.1 %copy-start.5 = (f32[1,4,16,512]{3,2,1,0:T(8,128)S(1)}, f32[1,4,16,512]{3,2,1,0:T(8,128)}, u32[]{:S(2)}) copy-start(f32[1,4,16,512]{3,2,1,0:T(8,128)} %copy-done.4) | copy-start | bytes 393220
  138.3 22.5 %all-to-all-start.1 = ((f32[16,1,4096]{2,1,0:T(1,128)}), f32[16,1,4096]{2,1,0:T(1,128)S(1)}, u32[]{:S(2)}, u32[]{:S(2)}) async-start(f32[16,1,4096]{2,1,0:T(1,128)} %reshape.345), calls=%async_computation.1 | async-start | bytes 524288 | tf_op jit(solution)/shard_map/all_to_all | solution.py:20
  166.4 1.8 %copy-start.9 = (f32[1,4,16,256]{3,2,1,0:T(8,128)S(1)}, f32[1,4,16,256]{3,2,1,0:T(8,128)}, u32[]{:S(2)}) copy-start(f32[1,4,16,256]{3,2,1,0:T(8,128)} %copy-done.8) | copy-start | bytes 196612
  166.5 2.8 %copy-start.7 = (f32[1,4,16,256]{3,2,1,0:T(8,128)S(1)}, f32[1,4,16,256]{3,2,1,0:T(8,128)}, u32[]{:S(2)}) copy-start(f32[1,4,16,256]{3,2,1,0:T(8,128)} %copy-done.6) | copy-start | bytes 196612
  167.4 1.9 %copy-start.11 = (f32[1,4,16,256]{3,2,1,0:T(8,128)S(1)}, f32[1,4,16,256]{3,2,1,0:T(8,128)}, u32[]{:S(2)}) copy-start(f32[1,4,16,256]{3,2,1,0:T(8,128)} %copy-done.10) | copy-start | bytes 196612
  167.4 1.9 %copy-start.17 = (f32[1,4,16,256]{3,2,1,0:T(8,128)S(1)}, f32[1,4,16,256]{3,2,1,0:T(8,128)}, u32[]{:S(2)}) copy-start(f32[1,4,16,256]{3,2,1,0:T(8,128)} %get-tuple-element.28) | copy-start | bytes 196612
  167.4 1.9 %copy-start.18 = (f32[1,4,16,256]{3,2,1,0:T(8,128)S(1)}, f32[1,4,16,256]{3,2,1,0:T(8,128)}, u32[]{:S(2)}) copy-start(f32[1,4,16,256]{3,2,1,0:T(8,128)} %get-tuple-element.43) | copy-start | bytes 196612
  167.4 1.9 %copy-start.20 = (f32[1,1,16,256]{3,2,1,0:T(8,128)S(1)}, f32[1,1,16,256]{3,2,1,0:T(8,128)}, u32[]{:S(2)}) copy-start(f32[1,1,16,256]{3,2,1,0:T(8,128)} %get-tuple-element.30) | copy-start | bytes 49156
  167.4 1.9 %copy-start.21 = (f32[1,1,16,256]{3,2,1,0:T(8,128)S(1)}, f32[1,1,16,256]{3,2,1,0:T(8,128)}, u32[]{:S(2)}) copy-start(f32[1,1,16,256]{3,2,1,0:T(8,128)} %get-tuple-element.33) | copy-start | bytes 49156
  167.5 1.9 %copy-start.22 = (f32[1,1,16,256]{3,2,1,0:T(8,128)S(1)}, f32[1,1,16,256]{3,2,1,0:T(8,128)}, u32[]{:S(2)}) copy-start(f32[1,1,16,256]{3,2,1,0:T(8,128)} %get-tuple-element.49) | copy-start | bytes 49156
  167.5 1.9 %copy-start.23 = (f32[1,1,16,256]{3,2,1,0:T(8,128)S(1)}, f32[1,1,16,256]{3,2,1,0:T(8,128)}, u32[]{:S(2)}) copy-start(f32[1,1,16,256]{3,2,1,0:T(8,128)} %get-tuple-element.50) | copy-start | bytes 49156
  167.5 2.0 %copy-start = (f32[2,1,4,16,512]{4,3,2,1,0:T(8,128)S(1)}, f32[2,1,4,16,512]{4,3,2,1,0:T(8,128)}, u32[]{:S(2)}) copy-start(f32[2,1,4,16,512]{4,3,2,1,0:T(8,128)} %param.3) | copy-start | bytes 786436
  167.5 2.0 %copy-start.16 = (f32[2,1,4,16,512]{4,3,2,1,0:T(8,128)S(1)}, f32[2,1,4,16,512]{4,3,2,1,0:T(8,128)}, u32[]{:S(2)}) copy-start(f32[2,1,4,16,512]{4,3,2,1,0:T(8,128)} %param.4) | copy-start | bytes 786436
